TPU v7x, 128 devices: a whole 4x4x4 slice. The times are simulated.
128 devices in a mesh: query: 4 (over z_lo, core), lib: 32 (over x, y, z_hi).
Axes of the slice: x: 4, y: 4, z: 4 (z_hi: 2, z_lo: 2; z = z_hi * 2 + z_lo), core: 2. Of those that a mesh axis runs over, the one named last changes fastest.
Arguments:
- queries: bfloat16 [4096, 2048], P(('query', 'lib')), may hold values from -64 to 64
- query_bucket: int32 [4096], P(('query', 'lib')), may hold values from 0 to 63, as said below
- library: bfloat16 [98304, 2048], P(('lib', 'query')), may hold values from -64 to 64
- library_time: bfloat16 [98304], P(('lib', 'query')), may hold values from 0 to 2
- library_bucket: int32 [98304], P(('lib', 'query')), may hold values from 0 to 63, as said below
Outputs:
- expected_spectra: bfloat16 [4096, 2048], P(('query', 'lib'))
- expected_time: float32 [4096], P(('query', 'lib'))
- log_evidence: float32 [4096], P(('query', 'lib'))
Inputs may be any that keep to these rules, and one draw needn't show every extreme that they name: `query_bucket`: library entries whose bucket differs from a query's by at most one are that query's candidates; the queries held by the devices at index i of lib lie in buckets 2 i and 2 i + 1. `library_bucket`: the library entries of every device hold each of the 64 buckets exactly 3072 // 256 times.
All inputs are finite; a program needn't handle non-finite values.
Results may differ from a plain program's by a relative error of at most 0.003.
Values may be sent and summed in bfloat16 or wider, within the bound.
A program may use at most 128 MiB of HBM per device.

v0:
```python
import jax
import jax.numpy as jnp
from jax import lax
from jax.sharding import PartitionSpec as P

SHARPNESS = 448


def entry_scale(spectra_rows):
    return lax.rsqrt(jnp.mean(jnp.square(spectra_rows.astype(jnp.float32)), axis=1) + 1e-06)


def scaled_scores(query_block, query_scale, block_bucket, entries, entry_bucket):
    products = lax.dot_general(
        query_block, entries, (((1,), (1,)), ((), ())), preferred_element_type=jnp.float32
    )
    inside = jnp.abs(block_bucket[:, None] - entry_bucket[None, :]) <= 1
    return jnp.where(
        inside, products * query_scale[:, None] * entry_scale(entries)[None, :], -jnp.inf
    )


def finish(spectra_sum, totals, time_sum, own_maxima):
    expected = (spectra_sum / totals[:, None]).astype(jnp.bfloat16)
    return (expected, time_sum / totals, own_maxima + jnp.log(totals))


def per_device(queries, query_bucket, library, library_time, library_bucket):
    own_rows = queries.shape[0]
    bin_count = queries.shape[1]
    query_block, block_bucket = (
        lax.all_gather(queries, "lib", axis=0, tiled=True),
        lax.all_gather(query_bucket, "lib", axis=0, tiled=True),
    )
    query_scale = entry_scale(query_block) * (SHARPNESS / bin_count)
    entries, entry_time, entry_bucket = (
        lax.all_gather(library, "query", axis=0, tiled=True),
        lax.all_gather(library_time, "query", axis=0, tiled=True),
        lax.all_gather(library_bucket, "query", axis=0, tiled=True),
    )
    scores = scaled_scores(query_block, query_scale, block_bucket, entries, entry_bucket)
    maxima = lax.pmax(jnp.max(scores, axis=1), "lib")
    weights = jnp.exp(scores - maxima[:, None]).astype(jnp.bfloat16)
    total_part = jnp.sum(weights.astype(jnp.float32), axis=1)
    spectra_part = jnp.dot(weights, entries, preferred_element_type=jnp.float32)
    time_part = jnp.dot(weights, entry_time, preferred_element_type=jnp.float32)
    first_row = lax.axis_index("lib") * own_rows
    total_all, time_all = lax.psum((total_part, time_part), "lib")
    spectra_sum = lax.psum_scatter(spectra_part, "lib", scatter_dimension=0, tiled=True)
    totals = lax.dynamic_slice_in_dim(total_all, first_row, own_rows)
    time_sum = lax.dynamic_slice_in_dim(time_all, first_row, own_rows)
    own_maxima = lax.dynamic_slice_in_dim(maxima, first_row, own_rows)
    return finish(spectra_sum, totals, time_sum, own_maxima)


def solution(mesh):
    placed = (
        P(("query", "lib"), None),
        P(("query", "lib")),
        P(("lib", "query"), None),
        P(("lib", "query")),
        P(("lib", "query")),
    )
    return jax.shard_map(
        per_device,
        mesh=mesh,
        in_specs=placed,
        out_specs=(P(("query", "lib"), None), P(("query", "lib")), P(("query", "lib"))),
        check_vma=False,
    )
```

profile of v0, /device:TPU:0, one launch (start us, length us, event | category | flops | bytes accessed | tf_op | source)
XLA Modules:
  0.0 572.3 jit_solution(1006789328680344113)
XLA Ops:
  7.2 0.0 all-gather.5.cloned.1.call-start
  7.2 0.7 all-gather.5.cloned.1.call-update
  7.9 0.0 all-gather.7.cloned.1.call-start
  7.9 0.7 all-gather.7.cloned.1.call-update
  8.6 0.0 reduce-scatter.2.cloned.1.call-start
  8.7 0.7 reshape.24
  9.4 1.2 dynamic-slice
  11.3 0.9 dynamic-update-slice
  12.2 21.3 %all-reduce = s32[1024]{0:T(1024)S(1)} all-reduce(s32[1024]{0:T(1024)S(1)} %dynamic-update-slice), channel_id=1, replica_groups=mesh['query'=4,'lib'=32] {'lib'}, use_global_device_ids=true, to_apply=%add | all-reduce | flops 1024 | bytes 8192
  33.5 5.2 all-gather
  38.7 57.0 %all-gather.5.cloned.1.call-done = bf16[1024,2048]{1,0:T(8,128)(2,1)} async-done(((bf16[32,2048]{1,0:T(8,128)(2,1)}), bf16[1024,2048]{1,0:T(8,128)(2,1)}) %all-gather.5.cloned.1.call-update) | async-done | bytes 4194320 | tf_op jit(solution)/shard_map/all_gather | solution.py:32
  95.7 3.1 multiply_reduce_fusion.1
  98.8 109.7 %all-gather.7.cloned.1.call-done = bf16[3072,2048]{1,0:T(8,128)(2,1)} async-done(((bf16[768,2048]{1,0:T(8,128)(2,1)}), bf16[3072,2048]{1,0:T(8,128)(2,1)}) %all-gather.7.cloned.1.call-update) | async-done | bytes 12582928 | tf_op jit(solution)/shard_map/all_gather | solution.py:37
  208.4 0.0 copy-start.1
  208.4 7.2 %multiply_reduce_fusion = f32[3072]{0:T(1024)S(1)} fusion(bf16[3072,2048]{1,0:T(8,128)(2,1)} %all-gather.7.cloned.1.call-done), kind=kLoop, calls=%fused_computation | loop fusion | flops 18871296 | bytes 12595200 | tf_op jit(solution)/shard_map/reduce_sum | solution.py:10
  215.7 0.0 copy-done.1
  215.7 19.3 %fusion = (f32[1024]{0:T(1024)S(1)}, f32[1024,3072]{1,0:T(8,128)}) fusion(f32[3072]{0:T(1024)S(1)} %add_rsqrt_fusion, f32[1024]{0:T(1024)S(1)} %rsqrt_multiply_fusion, s32[3072]{0:T(1024)S(1)} %bitcast.10, s32[1024]{0:T(1024)S(1)} %all-reduce, bf16[1024,2048]{1,0:T(8,128)(2,1)S(1)} %copy-done.1, bf16[3072,2048]{1,0:T(8,128)(2,1)} %all-gather.7.cloned.1.call-done), kind=kOutput, calls=%fused_computation.6 | convolution fusion | flops 12906920960 | bytes 29396992 | tf_op jit(solution)/shard_map/dot_general | solution.py:14
  235.0 96.7 %pmax.7 = f32[1024]{0:T(1024)S(1)} all-reduce(f32[1024]{0:T(1024)S(1)} %get-tuple-element.9), channel_id=1, replica_groups=mesh['query'=4,'lib'=32] {'lib'}, use_global_device_ids=true, to_apply=%region_3.4 | all-reduce | flops 1024 | bytes 8192 | tf_op jit(solution)/shard_map/pmax | solution.py:42
  331.7 8.3 %convert_reduce_fusion = (f32[1024]{0:T(1024)S(1)}, bf16[1024,3072]{1,0:T(8,128)(2,1)S(1)}) fusion(f32[1024]{0:T(1024)S(1)} %pmax.7, f32[3072]{0:T(1024)S(1)} %add_rsqrt_fusion, f32[1024,3072]{1,0:T(8,128)} %get-tuple-element.10, f32[1024]{0:T(1024)S(1)} %rsqrt_multiply_fusion, s32[3072]{0:T(1024)S(1)} %bitcast.11, s32[1024]{0:T(1024)S(1)} %all-reduce), kind=kLoop, calls=%fused_computation.1 | loop fusion | flops 31456256 | bytes 18915328 | tf_op jit(solution)/shard_map/reduce_sum | solution.py:44
  339.9 0.0 copy-start
  340.0 2.7 copy-done
  342.6 0.0 copy-start.2
  342.6 16.9 %fusion.1 = f32[1024,2048]{1,0:T(8,128)} fusion(bf16[1024,3072]{1,0:T(8,128)(2,1)S(1)} %get-tuple-element.8, bf16[3072,2048]{1,0:T(8,128)(2,1)} %all-gather.7.cloned.1.call-done), kind=kOutput, calls=%fused_computation.12 | convolution fusion | flops 12884901888 | bytes 27262976 | tf_op jit(solution)/shard_map/dot_general | solution.py:45
  359.5 0.0 reduce-scatter.2.cloned.1.call-update
  359.6 0.0 copy-done.2
  359.6 5.2 all-gather.1
  364.8 4.5 fusion.2
  369.3 90.5 %all-reduce.1 = (f32[1024]{0:T(1024)S(1)}, f32[1024]{0:T(1024)S(1)}) all-reduce(f32[1024]{0:T(1024)S(1)} %get-tuple-element.7, f32[1024]{0:T(1024)S(1)} %bitcast.13), channel_id=1, replica_groups=mesh['query'=4,'lib'=32] {'lib'}, use_global_device_ids=true, to_apply=%region_6.7 | all-reduce | flops 2048 | bytes 16384 | tf_op jit(solution)/shard_map/psum | solution.py:48
  459.8 0.6 log_add_fusion
  460.4 0.6 dynamic-slice_divide_fusion
  461.0 103.1 %reduce-scatter.2.cloned.1.call-done = f32[32,2048]{1,0:T(8,128)} async-done(((f32[1024,2048]{1,0:T(8,128)}), f32[32,2048]{1,0:T(8,128)}) %reduce-scatter.2.cloned.1.call-update) | async-done | bytes 262160 | tf_op jit(solution)/shard_map/reduce_scatter | solution.py:49
  564.1 1.7 divide_convert_fusion
  (4 shorter events, 0.0 us)
Async XLA Ops:
  7.2 88.5 %all-gather.5.cloned.1.call-start = ((), (), s32[]{:S(2)}) async-start(), calls=%async_computation.1 | async-start | bytes 4325376 | tf_op jit(solution)/shard_map/all_gather | solution.py:32
  7.9 200.5 %all-gather.7.cloned.1.call-start = ((), (), s32[]{:S(2)}) async-start(), calls=%async_computation.2 | async-start | bytes 15728640 | tf_op jit(solution)/shard_map/all_gather | solution.py:37
  8.6 555.5 %reduce-scatter.2.cloned.1.call-start = ((), (), s32[]{:S(2)}) async-start(), calls=%async_computation.3 | async-start | bytes 8650752 | tf_op jit(solution)/shard_map/reduce_scatter | solution.py:49
  208.4 7.3 %copy-start.1 = (bf16[1024,2048]{1,0:T(8,128)(2,1)S(1)}, bf16[1024,2048]{1,0:T(8,128)(2,1)}, u32[]{:S(2)}) copy-start(bf16[1024,2048]{1,0:T(8,128)(2,1)} %all-gather.5.cloned.1.call-done) | copy-start | bytes 12582916
  339.9 2.7 copy-start
  342.6 17.0 %copy-start.2 = (bf16[768]{0:T(1024)(128)(2,1)S(1)}, bf16[768]{0:T(1024)(128)(2,1)}, u32[]{:S(2)}) copy-start(bf16[768]{0:T(1024)(128)(2,1)} %param.8) | copy-start | bytes 4612
Sparse Core Ops, SparseCore 0:
  11.0 84.6 all-gather.4
  97.4 111.0 all-gather.6
  359.7 204.3 reduce-scatter.1
where the time goes:
time: 573 us; the launch traced here: 572 us
  waiting for transfers between devices  271 us (47%)
  blocking collectives  219 us (38%)
  matrix products  40.7 us (7%)
  other arithmetic  21.5 us (4%)
  between operations  14.5 us (3%)
    all_gather x1, waiting for transfers between devices, per_device(): lax.all_gather(library, 'query', axis=0, tiled=True)  110 us
    reduce_scatter x1, waiting for transfers between devices, per_device(): lax.psum_scatter(spectra_part, 'lib', scatter_dimension=0, tiled=True)  103 us
    pmax x1, blocking collectives, per_device(): maxima = lax.pmax(jnp.max(scores, axis=1), 'lib')  96.7 us
    psum x1, blocking collectives, per_device(): total_all, time_all = lax.psum((total_part, time_part), 'lib')  90.5 us
    all_gather x1, waiting for transfers between devices, per_device(): lax.all_gather(queries, 'lib', axis=0, tiled=True)  57 us
    unnamed x1, blocking collectives  21.3 us
    dot_general x1, matrix products, scaled_scores(): lax.dot_general(query_block, entries, (((1,), (1,)), ((), ())), preferred...  19.3 us
    dot_general x1, matrix products, per_device(): spectra_part = jnp.dot(weights, entries, preferred_element_type=jnp.float32)  16.9 us
  transfers between devices with their start and end apart: 3, of which 3 were waited for; matrix products, arithmetic and copies ran while one was open for 2% of the time, Pallas kernels for 0%

commit v1 on v0

--- a/solution.py
+++ b/solution.py
@@ -4,6 +4,11 @@
 from jax.sharding import PartitionSpec as P
 
 SHARPNESS = 448
+
+
+def swapped_in(value, axis, dim):
+    sent = jnp.stack([value] * lax.axis_size(axis))
+    return jnp.concatenate(lax.all_to_all(sent, axis, 0, 0), axis=dim)
 
 
 def entry_scale(spectra_rows):
@@ -29,7 +34,7 @@
     own_rows = queries.shape[0]
     bin_count = queries.shape[1]
     query_block, block_bucket = (
-        lax.all_gather(queries, "lib", axis=0, tiled=True),
+        swapped_in(queries, "lib", 0),
         lax.all_gather(query_bucket, "lib", axis=0, tiled=True),
     )
     query_scale = entry_scale(query_block) * (SHARPNESS / bin_count)

time: 573 us -> 535 us (0.934)
  waiting for transfers between devices: 271 us -> 178 us
  blocking collectives: 219 us -> 262 us
  starting transfers between devices: 0.11 us -> 11 us
    all_gather x1 -> x0, waiting for transfers between devices: 57 us -> none  [per_device(): lax.all_gather(queries, 'lib', axis=0, tiled=True)]
    unnamed x1, blocking collectives: 21.3 us -> 63.3 us
    all_gather x1, waiting for transfers between devices: 110 us -> 74.4 us  [per_device(): lax.all_gather(library, 'query', axis=0, tiled=True)]
    all_to_all x0 -> x1, starting transfers between devices: none -> 10.9 us  [swapped_in(): return jnp.concatenate(lax.all_to_all(sent, axis, 0, 0), axis=dim)]
  transfers between devices with their start and end apart: 3 -> 3, of which waited for: 3 -> 2; matrix products, arithmetic and copies ran while one was open for 2% -> 2% of each run, Pallas kernels for 0% -> 0%
where the time goes in v1:
time: 535 us
  blocking collectives  262 us (49%)
  waiting for transfers between devices  178 us (33%)
  matrix products  41.6 us (8%)
  other arithmetic  21.2 us (4%)
  between operations  14.9 us (3%)
  starting transfers between devices  11 us (2%)
  local copies, waits for them, and re-layouts  6.98 us (1%)
    reduce_scatter x1, waiting for transfers between devices, per_device(): lax.psum_scatter(spectra_part, 'lib', scatter_dimension=0, tiled=True)  103 us
    pmax x1, blocking collectives, per_device(): maxima = lax.pmax(jnp.max(scores, axis=1), 'lib')  96.9 us
    psum x1, blocking collectives, per_device(): total_all, time_all = lax.psum((total_part, time_part), 'lib')  91 us
    all_gather x1, waiting for transfers between devices, per_device(): lax.all_gather(library, 'query', axis=0, tiled=True)  74.4 us
    unnamed x1, blocking collectives  63.3 us
    dot_general x1, matrix products, scaled_scores(): lax.dot_general(query_block, entries, (((1,), (1,)), ((), ())), preferred...  20.2 us
    dot_general x1, matrix products, per_device(): spectra_part = jnp.dot(weights, entries, preferred_element_type=jnp.float32)  16.9 us
    all_to_all x1, starting transfers between devices, swapped_in(): return jnp.concatenate(lax.all_to_all(sent, axis, 0, 0), axis=dim)  10.9 us
  transfers between devices with their start and end apart: 3, of which 2 were waited for; matrix products, arithmetic and copies ran while one was open for 2% of the time, Pallas kernels for 0%

profile of v1, /device:TPU:0, one launch (start us, length us, event | category | flops | bytes accessed | tf_op | source)
XLA Modules:
  0.0 534.9 jit_solution(1883145540416498683)
XLA Ops:
  7.2 0.0 copy-start.4
  7.2 0.0 copy-start.1
  7.2 0.0 copy-start.3
  7.2 0.0 all-gather.4.cloned.1.call-start
  7.2 0.7 all-gather.4.cloned.1.call-update
  7.9 3.4 stack.2
  11.3 10.9 %all-to-all-start = ((bf16[32,32,2048]{2,1,0:T(8,128)(2,1)}), bf16[32,32,2048]{2,1,0:T(8,128)(2,1)}, u32[]{:S(2)}, u32[]{:S(2)}) async-start(bf16[32,32,2048]{2,1,0:T(8,128)(2,1)} %stack.2), calls=%async_computation | async-start | bytes 8388608 | tf_op jit(solution)/shard_map/all_to_all | solution.py:11
  22.2 0.0 reduce-scatter.2.cloned.1.call-start
  22.3 0.0 copy-done.1
  22.3 0.0 copy-done.4
  22.3 0.6 dynamic-slice
  23.6 0.0 copy-done.3
  23.6 0.2 dynamic-update-slice
  23.8 63.3 %all-reduce = s32[1024]{0:T(1024)S(1)} all-reduce(s32[1024]{0:T(1024)S(1)} %dynamic-update-slice), channel_id=1, replica_groups=mesh['query'=4,'lib'=32] {'lib'}, use_global_device_ids=true, to_apply=%add | all-reduce | flops 1024 | bytes 8192
  87.1 5.4 %all-gather = s32[4,1,768]{2,1,0:T(1,128)S(1)} all-gather(s32[1,1,768]{2,1,0:T(1,128)S(1)} %reshape.41), channel_id=1, replica_groups=mesh['query'=4,'lib'=32] {'query'}, dimensions={0}, use_global_device_ids=true | all-gather | bytes 15360 | tf_op jit(solution)/shard_map/all_gather | solution.py:44
  92.4 0.0 all-to-all-done
  92.4 3.1 multiply_reduce_fusion.1
  95.5 0.1 mul.34
  95.6 74.4 %all-gather.4.cloned.1.call-done = bf16[3072,2048]{1,0:T(8,128)(2,1)} async-done(((bf16[768,2048]{1,0:T(8,128)(2,1)}), bf16[3072,2048]{1,0:T(8,128)(2,1)}) %all-gather.4.cloned.1.call-update) | async-done | bytes 12582928 | tf_op jit(solution)/shard_map/all_gather | solution.py:42
  170.0 7.1 %multiply_reduce_fusion = f32[3072]{0:T(1024)S(1)} fusion(bf16[3072,2048]{1,0:T(8,128)(2,1)} %all-gather.4.cloned.1.call-done), kind=kLoop, calls=%fused_computation | loop fusion | flops 18871296 | bytes 12595200 | tf_op jit(solution)/shard_map/reduce_sum | solution.py:15
  177.1 20.2 %fusion = (f32[1024]{0:T(1024)S(1)}, f32[1024,3072]{1,0:T(8,128)}) fusion(f32[3072]{0:T(1024)S(1)} %add_rsqrt_fusion, f32[1024]{0:T(1024)S(1)} %mul.34, s32[3072]{0:T(1024)S(1)} %bitcast.11, s32[1024]{0:T(1024)S(1)} %all-reduce, bf16[1024,2048]{1,0:T(8,128)(2,1)} %bitcast.2, bf16[3072,2048]{1,0:T(8,128)(2,1)} %all-gather.4.cloned.1.call-done), kind=kOutput, calls=%fused_computation.6 | convolution fusion | flops 12906920960 | bytes 29396992 | tf_op jit(solution)/shard_map/dot_general | solution.py:19
  197.3 96.9 %pmax.7 = f32[1024]{0:T(1024)S(1)} all-reduce(f32[1024]{0:T(1024)S(1)} %get-tuple-element.9), channel_id=1, replica_groups=mesh['query'=4,'lib'=32] {'lib'}, use_global_device_ids=true, to_apply=%region_3.4 | all-reduce | flops 1024 | bytes 8192 | tf_op jit(solution)/shard_map/pmax | solution.py:47
  294.2 8.2 %convert_reduce_fusion = (f32[1024]{0:T(1024)S(1)}, bf16[1024,3072]{1,0:T(8,128)(2,1)S(1)}) fusion(f32[1024]{0:T(1024)S(1)} %pmax.7, f32[3072]{0:T(1024)S(1)} %add_rsqrt_fusion, f32[1024,3072]{1,0:T(8,128)} %get-tuple-element.10, f32[1024]{0:T(1024)S(1)} %mul.34, s32[3072]{0:T(1024)S(1)} %bitcast.12, s32[1024]{0:T(1024)S(1)} %all-reduce), kind=kLoop, calls=%fused_computation.1 | loop fusion | flops 31456256 | bytes 18915328 | tf_op jit(solution)/shard_map/reduce_sum | solution.py:49
  302.4 0.0 copy-start
  302.4 2.7 copy-done
  305.0 0.0 copy-start.2
  305.0 16.9 %fusion.1 = f32[1024,2048]{1,0:T(8,128)} fusion(bf16[1024,3072]{1,0:T(8,128)(2,1)S(1)} %get-tuple-element.8, bf16[3072,2048]{1,0:T(8,128)(2,1)} %all-gather.4.cloned.1.call-done), kind=kOutput, calls=%fused_computation.12 | convolution fusion | flops 12884901888 | bytes 27262976 | tf_op jit(solution)/shard_map/dot_general | solution.py:50
  322.0 0.0 reduce-scatter.2.cloned.1.call-update
  322.0 0.0 copy-done.2
  322.0 5.2 all-gather.1
  327.2 4.5 fusion.2
  331.7 91.0 %all-reduce.1 = (f32[1024]{0:T(1024)S(1)}, f32[1024]{0:T(1024)S(1)}) all-reduce(f32[1024]{0:T(1024)S(1)} %get-tuple-element.7, f32[1024]{0:T(1024)S(1)} %bitcast.14), channel_id=1, replica_groups=mesh['query'=4,'lib'=32] {'lib'}, use_global_device_ids=true, to_apply=%region_6.7 | all-reduce | flops 2048 | bytes 16384 | tf_op jit(solution)/shard_map/psum | solution.py:53
  422.7 0.6 log_add_fusion
  423.3 0.6 dynamic-slice_divide_fusion
  423.9 102.5 %reduce-scatter.2.cloned.1.call-done = f32[32,2048]{1,0:T(8,128)} async-done(((f32[1024,2048]{1,0:T(8,128)}), f32[32,2048]{1,0:T(8,128)}) %reduce-scatter.2.cloned.1.call-update) | async-done | bytes 262160 | tf_op jit(solution)/shard_map/reduce_scatter | solution.py:54
  526.4 1.7 divide_convert_fusion
  (5 shorter events, 0.0 us)
Async XLA Ops:
  7.2 15.1 %copy-start.4 = (u32[128]{0:T(128)S(1)}, u32[128]{0:T(128)}, u32[]{:S(2)}) copy-start(u32[128]{0:T(128)} %constant.30) | copy-start | bytes 1540
  7.2 15.1 %copy-start.1 = (s32[768]{0:T(1024)S(1)}, s32[768]{0:T(1024)}, u32[]{:S(2)}) copy-start(s32[768]{0:T(1024)} %param.9) | copy-start | bytes 9220
  7.2 16.4 %copy-start.3 = (s32[32]{0:T(128)S(1)}, s32[32]{0:T(128)}, u32[]{:S(2)}) copy-start(s32[32]{0:T(128)} %param.6) | copy-start | bytes 388
  7.2 162.8 %all-gather.4.cloned.1.call-start = ((), (), s32[]{:S(2)}) async-start(), calls=%async_computation.2 | async-start | bytes 15728640 | tf_op jit(solution)/shard_map/all_gather | solution.py:42
  11.3 81.1 %all-to-all-start = ((bf16[32,32,2048]{2,1,0:T(8,128)(2,1)}), bf16[32,32,2048]{2,1,0:T(8,128)(2,1)}, u32[]{:S(2)}, u32[]{:S(2)}) async-start(bf16[32,32,2048]{2,1,0:T(8,128)(2,1)} %stack.2), calls=%async_computation | async-start | bytes 8388608 | tf_op jit(solution)/shard_map/all_to_all | solution.py:11
  22.2 504.2 %reduce-scatter.2.cloned.1.call-start = ((), (), s32[]{:S(2)}) async-start(), calls=%async_computation.3 | async-start | bytes 8650752 | tf_op jit(solution)/shard_map/reduce_scatter | solution.py:54
  302.4 2.7 copy-start
  305.0 17.0 %copy-start.2 = (bf16[768]{0:T(1024)(128)(2,1)S(1)}, bf16[768]{0:T(1024)(128)(2,1)}, u32[]{:S(2)}) copy-start(bf16[768]{0:T(1024)(128)(2,1)} %param.8) | copy-start | bytes 4612
Sparse Core Ops, SparseCore 0:
  9.7 160.2 all-gather.3
  322.1 204.2 reduce-scatter.1
